TPU v7x, 128 devices: a whole 4x4x4 slice. The times are simulated.
128 devices in a mesh: dp: 32 (over z, y, core), col: 4 (over x).
Axes of the slice: x: 4, y: 4, z: 4, core: 2. Of those that a mesh axis runs over, the one named last changes fastest.
Arguments:
- tokens: bfloat16 [32768, 8192], P('dp', 'col'), may hold values from -6 to 6
- out_grad: bfloat16 [32768, 8192], P(('dp', 'col')), may hold values from -24 to 24
- weight: float32 [8192, 8192], P('dp', 'col'), may hold values from -6 to 6
- second: float32 [8192, 8192], P('dp', 'col'), may hold values from 0.0001 to 0.001
- momentum: float32 [8192, 512], P(('dp', 'col')), may hold values from -0.12 to 0.12
- sign_seed: int32 [1], replicated, may hold values from 0 to 999999
- step_number: int32 [1], replicated, may hold values from 1 to 999999
Outputs:
- new_weight: float32 [8192, 8192], P('dp', 'col')
- new_second: float32 [8192, 8192], P('dp', 'col')
- new_momentum: float32 [8192, 512], P(('dp', 'col'))
All inputs are finite; a program needn't handle non-finite values.
Results may differ from a plain program's by a relative error of at most 0.00097.
Values may be sent and summed in bfloat16 or wider, within the bound.
A program may use at most 128 MiB of HBM per device.

v0:
```python
import jax
import jax.numpy as jnp
from jax import lax
from jax.sharding import Mesh
from jax.sharding import PartitionSpec as P

DP = ("dp_0", "dp_1", "dp_2")
DP_COL = ("dp_0", "dp_1", "dp_2", "col")


def split_up(x, dim, count):
    before, after = (x.shape[:dim], x.shape[dim + 1 :])
    return jnp.moveaxis(x.reshape(*before, count, -1, *after), dim, 0)


def sent_and_summed(x, axis, dim):
    count = lax.axis_size(axis)
    pieces = lax.all_to_all(split_up(x, dim, count), axis, 0, 0, tiled=True)
    return jnp.sum(pieces, axis=0)


def from_everyone(x, axis):
    copies = jnp.broadcast_to(x, (lax.axis_size(axis), *x.shape))
    return lax.all_to_all(copies, axis, split_axis=0, concat_axis=0, tiled=True)


def joined_along(pieces, dim):
    pieces = jnp.moveaxis(pieces, 0, dim)
    lengths = pieces.shape
    return pieces.reshape(*lengths[:dim], lengths[dim] * lengths[dim + 1], *lengths[dim + 2 :])


def gather_directly(x, axis, dim):
    pieces = from_everyone(x, axis)
    return joined_along(pieces, dim)


def sum_in_two_steps(x, axes, dim):
    far, near = axes
    own = sent_and_summed(split_up(x, dim, lax.axis_size(far)), near, dim + 1)
    return jnp.sum(lax.all_to_all(own, far, 0, 0, tiled=True), axis=0)


def sign_table(sign_seed, step_number, first_row, row_count, low_rank):
    row_ids = first_row + lax.iota(jnp.int32, row_count)
    col_ids = lax.iota(jnp.int32, low_rank)
    flat_index = row_ids[:, None] * low_rank + col_ids[None, :]
    hashed = flat_index * 747796405 + sign_seed[0] * 1664525 + step_number[0] * 1013904223
    hashed = hashed ^ hashed >> 16 & 65535
    hashed = hashed * 2127912213
    hashed = hashed ^ hashed >> 13 & 524287
    hashed = hashed * 1103515245
    hashed = hashed ^ hashed >> 16 & 65535
    low_bit = hashed >> 20 & 1
    return (1 - 2 * low_bit).astype(jnp.float32)


def contract(left_rows, right_rows):
    return lax.dot_general(
        left_rows, right_rows, (((0,), (0,)), ((), ())), preferred_element_type=jnp.float32
    )


def per_device(tokens, out_grad, weight, second, momentum, sign_seed, step_number):
    local_tokens, din_local = tokens.shape
    low_rank = momentum.shape[1]
    owner_rows = momentum.shape[0]
    inv_root = 1.0 / jnp.sqrt(jnp.float32(low_rank))
    col_position = lax.axis_index("col")
    sign_block = sign_table(sign_seed, step_number, col_position * din_local, din_local, low_rank)
    partial_sketch = (
        jnp.dot(tokens, sign_block.astype(jnp.bfloat16), preferred_element_type=jnp.float32)
        * inv_root
    )
    quarter = sent_and_summed(partial_sketch, "col", 0)
    sketch = quarter.astype(jnp.bfloat16)
    total_tokens = lax.axis_size(DP) * local_tokens
    data_count = lax.axis_size(DP)
    col_count = lax.axis_size("col")
    quarter_rows = out_grad.shape[0]
    grouped = out_grad.reshape(quarter_rows, data_count, col_count, owner_rows)
    grouped = jnp.transpose(grouped, (0, 2, 1, 3)).reshape(
        quarter_rows, col_count, data_count * owner_rows
    )
    regrouped = lax.all_to_all(grouped, "col", split_axis=1, concat_axis=0, tiled=True)
    regrouped = regrouped.reshape(quarter_rows * col_count, data_count * owner_rows)
    shard_sketch = gather_directly(sketch, "col", 0)
    projected = sum_in_two_steps(contract(regrouped, shard_sketch), (("dp_0", "dp_1"), "dp_2"), 0)
    projected = projected / jnp.float32(total_tokens)
    new_momentum = 0.8 * momentum + 0.2 * projected
    row_block = gather_directly(new_momentum, "col", 0)
    dense_grad = (
        lax.dot_general(
            row_block,
            sign_block,
            (((1,), (1,)), ((), ())),
            precision=lax.Precision.HIGHEST,
            preferred_element_type=jnp.float32,
        )
        * inv_root
    )
    new_second = 0.95 * second + 0.05 * dense_grad * dense_grad
    new_weight = weight - 0.5 * dense_grad / (jnp.sqrt(new_second) + 1e-08)
    return (new_weight, new_second, new_momentum)


def solution(mesh):
    torus = Mesh(mesh.devices.reshape(4, 4, 2, mesh.shape["col"]), ("dp_0", "dp_1", "dp_2", "col"))
    return jax.shard_map(
        per_device,
        mesh=torus,
        in_specs=(
            P(DP, "col"),
            P(DP_COL, None),
            P(DP, "col"),
            P(DP, "col"),
            P(DP_COL, None),
            P(),
            P(),
        ),
        out_specs=(P(DP, "col"), P(DP, "col"), P(DP_COL, None)),
        check_vma=False,
    )
```

profile of v0, /device:TPU:0, one launch (start us, length us, event | category | flops | bytes accessed | tf_op | source)
XLA Modules:
  0.0 196.9 jit_solution(12246148960320195151)
XLA Ops:
  1.9 6.4 %fusion.3 = f32[512,1024]{1,0:T(8,128)S(1)} fusion(bf16[1024,2048]{1,0:T(8,128)(2,1)} %param.7, s32[]{:T(128)} %bitcast.1, s32[]{:T(128)} %bitcast, s32[2048]{0:T(1024)S(1)} %add_multiply_fusion), kind=kOutput, calls=%fused_computation.9 | convolution fusion | flops 2170028032 | bytes 6299656 | tf_op jit(solution)/shard_map/dot_general | solution.py:72
  8.3 1.5 copy.33
  9.8 4.4 %all-to-all-start = ((f32[4,256,512]{1,2,0:T(8,128)}), f32[4,256,512]{1,2,0:T(8,128)S(1)}, u32[]{:S(2)}, u32[]{:S(2)}) async-start(f32[4,256,512]{1,2,0:T(8,128)} %bitcast.30), calls=%async_computation | async-start | bytes 4194304 | tf_op jit(solution)/shard_map/all_to_all | solution.py:18
  14.2 6.4 %copy.25 = bf16[256,8192]{0,1:T(8,128)(2,1)} copy(bf16[256,8192]{1,0:T(8,128)(2,1)} %param.8) | data formatting | bytes 8388608 | tf_op args[1]
  20.6 4.7 %copy.26 = bf16[256,4,32,64]{0,3,2,1:T(8,128)(2,1)} copy(bf16[256,4,32,64]{0,3,1,2:T(8,128)(2,1)} %bitcast.29) | data formatting | bytes 8388608 | tf_op jit(solution)/shard_map/transpose | solution.py:82
  25.3 15.2 %all-to-all-done = f32[4,256,512]{1,2,0:T(8,128)S(1)} async-done(((f32[4,256,512]{1,2,0:T(8,128)}), f32[4,256,512]{1,2,0:T(8,128)S(1)}, u32[]{:S(2)}, u32[]{:S(2)}) %all-to-all-start) | async-done | bytes 2097184 | tf_op jit(solution)/shard_map/all_to_all | solution.py:18
  40.5 4.9 %all-to-all-start.2 = ((bf16[256,4,2048]{0,2,1:T(8,128)(2,1)}), bf16[256,4,2048]{0,2,1:T(8,128)(2,1)}, u32[]{:S(2)}, u32[]{:S(2)}) async-start(bf16[256,4,2048]{0,2,1:T(8,128)(2,1)} %bitcast.27), calls=%async_computation.2 | async-start | bytes 8388608 | tf_op jit(solution)/shard_map/all_to_all | solution.py:85
  45.4 0.1 reduce_sum.27
  45.5 0.1 copy.24
  45.7 47.6 %all-to-all-done.2 = bf16[256,4,2048]{0,2,1:T(8,128)(2,1)} async-done(((bf16[256,4,2048]{0,2,1:T(8,128)(2,1)}), bf16[256,4,2048]{0,2,1:T(8,128)(2,1)}, u32[]{:S(2)}, u32[]{:S(2)}) %all-to-all-start.2) | async-done | bytes 4194336 | tf_op jit(solution)/shard_map/all_to_all | solution.py:85
  93.3 1.1 broadcast_in_dim.8
  94.4 3.5 %all-to-all-start.1 = ((bf16[4,256,512]{2,1,0:T(8,128)(2,1)}), bf16[4,256,512]{2,1,0:T(8,128)(2,1)S(1)}, u32[]{:S(2)}, u32[]{:S(2)}) async-start(bf16[4,256,512]{2,1,0:T(8,128)(2,1)} %broadcast_in_dim.8), calls=%async_computation.1 | async-start | bytes 2097152 | tf_op jit(solution)/shard_map/all_to_all | solution.py:24
  97.9 6.3 %copy.27 = bf16[4,256,1,2048]{3,1,0,2:T(8,128)(2,1)} copy(bf16[4,256,1,2048]{1,3,0,2:T(8,128)(2,1)} %bitcast.8) | data formatting | bytes 8388608 | tf_op jit(solution)/shard_map/all_to_all | solution.py:85
  104.2 7.0 %all-to-all-done.1 = bf16[4,256,512]{2,1,0:T(8,128)(2,1)S(1)} async-done(((bf16[4,256,512]{2,1,0:T(8,128)(2,1)}), bf16[4,256,512]{2,1,0:T(8,128)(2,1)S(1)}, u32[]{:S(2)}, u32[]{:S(2)}) %all-to-all-start.1) | async-done | bytes 1048608 | tf_op jit(solution)/shard_map/all_to_all | solution.py:24
  111.1 6.5 %convolution_bitcast_fusion = f32[2048,512]{0,1:T(8,128)} fusion(bf16[1024,512]{1,0:T(8,128)(2,1)S(1)} %bitcast.31, bf16[1024,2048]{1,0:T(8,128)(2,1)} %bitcast.26), kind=kOutput, calls=%fused_computation.4 | convolution fusion | flops 2147483648 | bytes 9437184 | tf_op jit(solution)/shard_map/dot_general | solution.py:59
  117.6 5.4 %copy.28 = f32[2048,512]{1,0:T(8,128)} copy(f32[2048,512]{0,1:T(8,128)} %convolution_bitcast_fusion) | data formatting | bytes 8388608 | tf_op jit(solution)/shard_map/dot_general | solution.py:59
  123.0 2.8 %copy.29 = f32[2,16,64,512]{3,2,1,0:T(8,128)S(1)} copy(f32[2,16,64,512]{3,2,0,1:T(8,128)} %bitcast.28) | data formatting | bytes 8388608 | tf_op jit(solution)/shard_map/transpose | solution.py:13
  125.8 8.2 %all_to_all.40 = f32[2,16,64,512]{3,2,1,0:T(8,128)} all-to-all(f32[2,16,64,512]{3,2,1,0:T(8,128)S(1)} %copy.29), channel_id=1, replica_groups=mesh['dp_0'=4,'dp_1'=4,'dp_2'=2,'col'=4] {'dp_2'}, dimensions={0} | all-to-all | bytes 8388608 | tf_op jit(solution)/shard_map/all_to_all | solution.py:18
  133.9 2.9 %reduce_sum.28 = f32[16,64,512]{2,1,0:T(8,128)S(1)} reduce(f32[2,16,64,512]{3,2,1,0:T(8,128)} %all_to_all.40, f32[]{:T(128)} %constant.21.clone.1), dimensions={0}, to_apply=%region_1.0 | reduce | flops 524288 | bytes 6291460 | tf_op jit(solution)/shard_map/reduce_sum | solution.py:19
  136.8 0.0 copy-start.1
  136.8 36.8 %all_to_all.41 = f32[16,64,512]{2,1,0:T(8,128)} all-to-all(f32[16,64,512]{2,1,0:T(8,128)S(1)} %reduce_sum.28), channel_id=1, replica_groups=mesh['dp_0'=4,'dp_1'=4,'dp_2'=2,'col'=4] {'dp_0','dp_1'}, dimensions={0} | all-to-all | bytes 4194304 | tf_op jit(solution)/shard_map/all_to_all | solution.py:41
  173.6 1.8 reduce_sum.29
  175.3 0.0 copy-done.1
  175.4 0.0 copy-start
  175.4 0.1 broadcast_in_dim.9
  175.5 11.1 %all_to_all.42 = f32[4,64,512]{2,1,0:T(8,128)S(1)} all-to-all(f32[4,64,512]{2,1,0:T(8,128)S(1)} %broadcast_in_dim.9), channel_id=1, replica_groups=mesh['dp_0'=4,'dp_1'=4,'dp_2'=2,'col'=4] {'col'}, dimensions={0} | all-to-all | bytes 1048576 | tf_op jit(solution)/shard_map/all_to_all | solution.py:24
  186.5 10.4 %divide_subtract_fusion = (f32[256,2048]{1,0:T(8,128)}, f32[256,2048]{1,0:T(8,128)}) fusion(f32[256,2048]{1,0:T(8,128)} %param.9, f32[256,2048]{1,0:T(8,128)} %param.10, f32[256,512]{1,0:T(8,128)S(1)} %bitcast.33, s32[]{:T(128)} %bitcast.1, s32[]{:T(128)} %bitcast, s32[2048]{0:T(1024)S(1)} %add_multiply_fusion), kind=kOutput, calls=%fused_computation.7 | convolution fusion | flops 3246915584 | bytes 8921096 | tf_op jit(solution)/shard_map/dot_general | solution.py:93
  196.9 0.0 copy-done
  (2 shorter events, 0.0 us)
Async XLA Ops:
  9.8 30.7 %all-to-all-start = ((f32[4,256,512]{1,2,0:T(8,128)}), f32[4,256,512]{1,2,0:T(8,128)S(1)}, u32[]{:S(2)}, u32[]{:S(2)}) async-start(f32[4,256,512]{1,2,0:T(8,128)} %bitcast.30), calls=%async_computation | async-start | bytes 4194304 | tf_op jit(solution)/shard_map/all_to_all | solution.py:18
  40.5 52.8 %all-to-all-start.2 = ((bf16[256,4,2048]{0,2,1:T(8,128)(2,1)}), bf16[256,4,2048]{0,2,1:T(8,128)(2,1)}, u32[]{:S(2)}, u32[]{:S(2)}) async-start(bf16[256,4,2048]{0,2,1:T(8,128)(2,1)} %bitcast.27), calls=%async_computation.2 | async-start | bytes 8388608 | tf_op jit(solution)/shard_map/all_to_all | solution.py:85
  94.4 16.7 %all-to-all-start.1 = ((bf16[4,256,512]{2,1,0:T(8,128)(2,1)}), bf16[4,256,512]{2,1,0:T(8,128)(2,1)S(1)}, u32[]{:S(2)}, u32[]{:S(2)}) async-start(bf16[4,256,512]{2,1,0:T(8,128)(2,1)} %broadcast_in_dim.8), calls=%async_computation.1 | async-start | bytes 2097152 | tf_op jit(solution)/shard_map/all_to_all | solution.py:24
  136.8 38.5 %copy-start.1 = (f32[64,512]{1,0:T(8,128)S(1)}, f32[64,512]{1,0:T(8,128)}, u32[]{:S(2)}) copy-start(f32[64,512]{1,0:T(8,128)} %param.11) | copy-start | bytes 393220
  175.4 21.6 %copy-start = (f32[64,512]{1,0:T(8,128)}, f32[64,512]{1,0:T(8,128)S(1)}, u32[]{:S(2)}) copy-start(f32[64,512]{1,0:T(8,128)S(1)} %multiply_add_fusion.1) | copy-start | bytes 393220
where the time goes:
time: 198 us; the launch traced here: 197 us
  waiting for transfers between devices  69.8 us (35%)
  blocking collectives  56 us (28%)
  local copies, waits for them, and re-layouts  28.3 us (14%)
  matrix products  23.3 us (12%)
  starting transfers between devices  12.8 us (6%)
  other arithmetic  4.8 us (2%)
  between operations  2.03 us (1%)
    all_to_all x1, waiting for transfers between devices, per_device(): lax.all_to_all(grouped, 'col', split_axis=1, concat_axis=0, tiled=True)  47.6 us
    all_to_all x1, blocking collectives, sum_in_two_steps(): return jnp.sum(lax.all_to_all(own, far, 0, 0, tiled=True), axis=0)  36.8 us
    all_to_all x1, waiting for transfers between devices, sent_and_summed(): pieces = lax.all_to_all(split_up(x, dim, count), axis, 0, 0, tiled=True)  15.2 us
    all_to_all x1, blocking collectives, from_everyone(): return lax.all_to_all(copies, axis, split_axis=0, concat_axis=0, tiled=True)  11.1 us
    dot_general x1, matrix products, per_device(): lax.dot_general(row_block, sign_block, (((1,), (1,)), ((), ())), precisio...  10.4 us
    all_to_all x1, blocking collectives, sent_and_summed(): pieces = lax.all_to_all(split_up(x, dim, count), axis, 0, 0, tiled=True)  8.17 us
    all_to_all x1, waiting for transfers between devices, from_everyone(): return lax.all_to_all(copies, axis, split_axis=0, concat_axis=0, tiled=True)  6.95 us
    dot_general x1, matrix products, contract(): lax.dot_general(left_rows, right_rows, (((0,), (0,)), ((), ())), preferre...  6.5 us
  transfers between devices with their start and end apart: 3, of which 3 were waited for; matrix products, arithmetic and copies ran while one was open for 9% of the time, Pallas kernels for 0%

commit v1 on v0

--- a/solution.py
+++ b/solution.py
@@ -82,7 +82,10 @@
     grouped = jnp.transpose(grouped, (0, 2, 1, 3)).reshape(
         quarter_rows, col_count, data_count * owner_rows
     )
-    regrouped = lax.all_to_all(grouped, "col", split_axis=1, concat_axis=0, tiled=True)
+    regrouped = jnp.concatenate(
+        lax.all_to_all(jnp.stack(jnp.split(grouped, lax.axis_size("col"), axis=1)), "col", 0, 0),
+        axis=0,
+    )
     regrouped = regrouped.reshape(quarter_rows * col_count, data_count * owner_rows)
     shard_sketch = gather_directly(sketch, "col", 0)
     projected = sum_in_two_steps(contract(regrouped, shard_sketch), (("dp_0", "dp_1"), "dp_2"), 0)

time: 198 us -> 190 us (0.960)
  waiting for transfers between devices: 69.8 us -> 63 us
  local copies, waits for them, and re-layouts: 28.3 us -> 25.4 us
  other arithmetic: 4.8 us -> 7.05 us
  matrix products: 23.3 us -> 21.3 us
    all_to_all x1, waiting for transfers between devices: 6.95 us -> 0.44 us  [from_everyone(): return lax.all_to_all(copies, axis, split_axis=0, concat_axis=0, tiled=True)]
    another operation x0 -> x1, other arithmetic: none -> 2.25 us  [per_device(): jnp.stack(jnp.split(grouped, lax.axis_size('col'), axis=1))]
    transpose x1, local copies, waits for them, and re-layouts: 4.74 us -> 2.49 us  [per_device(): jnp.transpose(grouped, (0, 2, 1, 3))]
    transpose x1, local copies, waits for them, and re-layouts: 2.75 us -> 0.7 us  [split_up(): return jnp.moveaxis(x.reshape(*before, count, -1, *after), dim, 0)]
  transfers between devices with their start and end apart: 3 -> 3, of which waited for: 3 -> 3; matrix products, arithmetic and copies ran while one was open for 9% -> 13% of each run, Pallas kernels for 0% -> 0%
where the time goes in v1:
time: 190 us; the launch traced here: 189 us
  waiting for transfers between devices  63 us (33%)
  blocking collectives  57.4 us (30%)
  local copies, waits for them, and re-layouts  25.4 us (13%)
  matrix products  21.3 us (11%)
  starting transfers between devices  12.7 us (7%)
  other arithmetic  7.05 us (4%)
  between operations  2.05 us (1%)
    all_to_all x1, waiting for transfers between devices, per_device(): lax.all_to_all(jnp.stack(jnp.split(grouped, lax.axis_size('col'), axis=1)...  47.7 us
    all_to_all x1, blocking collectives, sum_in_two_steps(): return jnp.sum(lax.all_to_all(own, far, 0, 0, tiled=True), axis=0)  36.8 us
    all_to_all x1, waiting for transfers between devices, sent_and_summed(): pieces = lax.all_to_all(split_up(x, dim, count), axis, 0, 0, tiled=True)  14.9 us
    all_to_all x1, blocking collectives, from_everyone(): return lax.all_to_all(copies, axis, split_axis=0, concat_axis=0, tiled=True)  12.5 us
    dot_general x1, matrix products, per_device(): lax.dot_general(row_block, sign_block, (((1,), (1,)), ((), ())), precisio...  10.4 us
    all_to_all x1, blocking collectives, sent_and_summed(): pieces = lax.all_to_all(split_up(x, dim, count), axis, 0, 0, tiled=True)  8.16 us
    unnamed x5, local copies, waits for them, and re-layouts  6.4 us
    all_to_all x1, local copies, waits for them, and re-layouts, per_device(): lax.all_to_all(jnp.stack(jnp.split(grouped, lax.axis_size('col'), axis=1)...  6.4 us
  transfers between devices with their start and end apart: 3, of which 3 were waited for; matrix products, arithmetic and copies ran while one was open for 13% of the time, Pallas kernels for 0%

profile of v1, /device:TPU:0, one launch (start us, length us, event | category | flops | bytes accessed | tf_op | source)
XLA Modules:
  0.0 189.0 jit_solution(401841918610471110)
XLA Ops:
  1.9 6.4 %fusion.3 = f32[512,1024]{1,0:T(8,128)S(1)} fusion(bf16[1024,2048]{1,0:T(8,128)(2,1)} %param.7, s32[]{:T(128)} %bitcast.11, s32[]{:T(128)} %bitcast.10, s32[2048]{0:T(1024)S(1)} %add_multiply_fusion), kind=kOutput, calls=%fused_computation.10 | convolution fusion | flops 2170028032 | bytes 6299656 | tf_op jit(solution)/shard_map/dot_general | solution.py:72
  8.3 1.5 copy.48
  9.8 4.4 %all-to-all-start.1 = ((f32[4,256,512]{1,2,0:T(8,128)}), f32[4,256,512]{1,2,0:T(8,128)S(1)}, u32[]{:S(2)}, u32[]{:S(2)}) async-start(f32[4,256,512]{1,2,0:T(8,128)} %bitcast.38), calls=%async_computation.1 | async-start | bytes 4194304 | tf_op jit(solution)/shard_map/all_to_all | solution.py:18
  14.2 6.4 %copy.33 = bf16[256,8192]{0,1:T(8,128)(2,1)} copy(bf16[256,8192]{1,0:T(8,128)(2,1)} %param.8) | data formatting | bytes 8388608 | tf_op args[1]
  20.6 2.5 %copy.34 = bf16[256,4,32,64]{0,3,2,1:T(8,128)(2,1)S(1)} copy(bf16[256,4,32,64]{0,3,1,2:T(8,128)(2,1)} %bitcast.37) | data formatting | bytes 8388608 | tf_op jit(solution)/shard_map/transpose | solution.py:82
  23.1 0.3 slice_bitcast_fusion.3
  23.4 2.2 %pad_maximum_fusion = bf16[4,256,1,2048]{1,3,2,0:T(8,128)(2,1)} fusion(bf16[1,256,1,2048]{1,3,2,0:T(8,128)(2,1)S(1)} %get-tuple-element.6, bf16[1,256,1,2048]{1,3,2,0:T(8,128)(2,1)S(1)} %get-tuple-element.7, bf16[1,256,1,2048]{1,3,2,0:T(8,128)(2,1)S(1)} %get-tuple-element.8, bf16[1,256,1,2048]{1,3,2,0:T(8,128)(2,1)S(1)} %get-tuple-element.5), kind=kLoop, calls=%fused_computation | loop fusion | flops 6291456 | bytes 8388608 | tf_op jit(solution)/shard_map/stack | solution.py:86
  25.6 14.9 %all-to-all-done.1 = f32[4,256,512]{1,2,0:T(8,128)S(1)} async-done(((f32[4,256,512]{1,2,0:T(8,128)}), f32[4,256,512]{1,2,0:T(8,128)S(1)}, u32[]{:S(2)}, u32[]{:S(2)}) %all-to-all-start.1) | async-done | bytes 2097184 | tf_op jit(solution)/shard_map/all_to_all | solution.py:18
  40.5 4.8 %all-to-all-start = ((bf16[4,256,1,2048]{1,3,2,0:T(8,128)(2,1)}), bf16[4,256,1,2048]{1,3,2,0:T(8,128)(2,1)}, u32[]{:S(2)}, u32[]{:S(2)}) async-start(bf16[4,256,1,2048]{1,3,2,0:T(8,128)(2,1)} %pad_maximum_fusion), calls=%async_computation | async-start | bytes 8388608 | tf_op jit(solution)/shard_map/all_to_all | solution.py:86
  45.4 0.1 reduce_sum.27
  45.5 0.1 copy.41
  45.7 47.7 %all-to-all-done = bf16[4,256,1,2048]{1,3,2,0:T(8,128)(2,1)} async-done(((bf16[4,256,1,2048]{1,3,2,0:T(8,128)(2,1)}), bf16[4,256,1,2048]{1,3,2,0:T(8,128)(2,1)}, u32[]{:S(2)}, u32[]{:S(2)}) %all-to-all-start) | async-done | bytes 4194336 | tf_op jit(solution)/shard_map/all_to_all | solution.py:86
  93.3 1.1 broadcast_in_dim.8
  94.4 3.5 %all-to-all-start.2 = ((bf16[4,256,512]{2,1,0:T(8,128)(2,1)}), bf16[4,256,512]{2,1,0:T(8,128)(2,1)S(1)}, u32[]{:S(2)}, u32[]{:S(2)}) async-start(bf16[4,256,512]{2,1,0:T(8,128)(2,1)} %broadcast_in_dim.8), calls=%async_computation.2 | async-start | bytes 2097152 | tf_op jit(solution)/shard_map/all_to_all | solution.py:24
  97.9 6.4 %copy.37 = bf16[4,256,1,2048]{3,1,0,2:T(8,128)(2,1)} copy(bf16[4,256,1,2048]{1,3,2,0:T(8,128)(2,1)} %all-to-all-done) | data formatting | bytes 8388608 | tf_op jit(solution)/shard_map/all_to_all | solution.py:86
  104.3 6.4 %copy.38 = bf16[2048,1024]{1,0:T(8,128)(2,1)} copy(bf16[2048,1024]{0,1:T(8,128)(2,1)} %bitcast.36) | data formatting | bytes 8388608 | tf_op jit(solution)/shard_map/dot_general | solution.py:59
  110.7 0.4 all-to-all-done.2
  111.1 4.5 %convolution_bitcast_fusion = f32[2,16,64,512]{3,2,0,1:T(8,128)S(1)} fusion(bf16[16,2,64,1024]{3,2,1,0:T(8,128)(2,1)} %bitcast.39, bf16[1024,512,1,1]{1,0,3,2:T(8,128)(2,1)S(1)} %bitcast.41), kind=kOutput, calls=%fused_computation.5 | convolution fusion | flops 2147483648 | bytes 9437184 | tf_op jit(solution)/shard_map/dot_general | solution.py:59
  115.7 0.7 copy.42
  116.4 8.2 %all_to_all.30 = f32[2,16,64,512]{3,2,1,0:T(8,128)} all-to-all(f32[2,16,64,512]{3,2,1,0:T(8,128)S(1)} %copy.42), channel_id=1, replica_groups=mesh['dp_0'=4,'dp_1'=4,'dp_2'=2,'col'=4] {'dp_2'}, dimensions={0} | all-to-all | bytes 8388608 | tf_op jit(solution)/shard_map/all_to_all | solution.py:18
  124.5 2.9 %reduce_sum.28 = f32[16,64,512]{2,1,0:T(8,128)S(1)} reduce(f32[2,16,64,512]{3,2,1,0:T(8,128)} %all_to_all.30, f32[]{:T(128)} %constant.21.clone.1), dimensions={0}, to_apply=%region_1.0 | reduce | flops 524288 | bytes 6291460 | tf_op jit(solution)/shard_map/reduce_sum | solution.py:19
  127.4 0.0 copy-start.1
  127.4 36.8 %all_to_all.31 = f32[16,64,512]{2,1,0:T(8,128)} all-to-all(f32[16,64,512]{2,1,0:T(8,128)S(1)} %reduce_sum.28), channel_id=1, replica_groups=mesh['dp_0'=4,'dp_1'=4,'dp_2'=2,'col'=4] {'dp_0','dp_1'}, dimensions={0} | all-to-all | bytes 4194304 | tf_op jit(solution)/shard_map/all_to_all | solution.py:41
  164.2 1.8 reduce_sum.29
  166.0 0.0 copy-done.1
  166.0 0.0 copy-start
  166.0 0.1 broadcast_in_dim.9
  166.1 12.5 %all_to_all.32 = f32[4,64,512]{2,1,0:T(8,128)S(1)} all-to-all(f32[4,64,512]{2,1,0:T(8,128)S(1)} %broadcast_in_dim.9), channel_id=1, replica_groups=mesh['dp_0'=4,'dp_1'=4,'dp_2'=2,'col'=4] {'col'}, dimensions={0} | all-to-all | bytes 1048576 | tf_op jit(solution)/shard_map/all_to_all | solution.py:24
  178.6 10.4 %divide_subtract_fusion = (f32[256,2048]{1,0:T(8,128)}, f32[256,2048]{1,0:T(8,128)}) fusion(f32[256,2048]{1,0:T(8,128)} %param.9, f32[256,2048]{1,0:T(8,128)} %param.10, f32[256,512]{1,0:T(8,128)S(1)} %bitcast.42, s32[]{:T(128)} %bitcast.11, s32[]{:T(128)} %bitcast.10, s32[2048]{0:T(1024)S(1)} %add_multiply_fusion), kind=kOutput, calls=%fused_computation.8 | convolution fusion | flops 3246915584 | bytes 8921096 | tf_op jit(solution)/shard_map/dot_general | solution.py:96
  189.0 0.0 copy-done
  (2 shorter events, 0.0 us)
Async XLA Ops:
  9.8 30.7 %all-to-all-start.1 = ((f32[4,256,512]{1,2,0:T(8,128)}), f32[4,256,512]{1,2,0:T(8,128)S(1)}, u32[]{:S(2)}, u32[]{:S(2)}) async-start(f32[4,256,512]{1,2,0:T(8,128)} %bitcast.38), calls=%async_computation.1 | async-start | bytes 4194304 | tf_op jit(solution)/shard_map/all_to_all | solution.py:18
  40.5 52.8 %all-to-all-start = ((bf16[4,256,1,2048]{1,3,2,0:T(8,128)(2,1)}), bf16[4,256,1,2048]{1,3,2,0:T(8,128)(2,1)}, u32[]{:S(2)}, u32[]{:S(2)}) async-start(bf16[4,256,1,2048]{1,3,2,0:T(8,128)(2,1)} %pad_maximum_fusion), calls=%async_computation | async-start | bytes 8388608 | tf_op jit(solution)/shard_map/all_to_all | solution.py:86
  94.4 16.8 %all-to-all-start.2 = ((bf16[4,256,512]{2,1,0:T(8,128)(2,1)}), bf16[4,256,512]{2,1,0:T(8,128)(2,1)S(1)}, u32[]{:S(2)}, u32[]{:S(2)}) async-start(bf16[4,256,512]{2,1,0:T(8,128)(2,1)} %broadcast_in_dim.8), calls=%async_computation.2 | async-start | bytes 2097152 | tf_op jit(solution)/shard_map/all_to_all | solution.py:24
  127.4 38.5 %copy-start.1 = (f32[64,512]{1,0:T(8,128)S(1)}, f32[64,512]{1,0:T(8,128)}, u32[]{:S(2)}) copy-start(f32[64,512]{1,0:T(8,128)} %param.11) | copy-start | bytes 393220
  166.0 23.0 %copy-start = (f32[64,512]{1,0:T(8,128)}, f32[64,512]{1,0:T(8,128)S(1)}, u32[]{:S(2)}) copy-start(f32[64,512]{1,0:T(8,128)S(1)} %multiply_add_fusion.1) | copy-start | bytes 393220
